TPU v7x, 32 devices: a whole 2x2x4 slice. The times are simulated.
32 devices in a mesh: mod: 4 (over z), frm: 2 (over x), ori: 4 (over y, core).
Axes of the slice: x: 2, y: 2, z: 4, core: 2. Of those that a mesh axis runs over, the one named last changes fastest.
Arguments:
- counts: int32 [512, 128, 128], P(('frm', 'ori'), 'mod'), may hold values from 0 to 8
- slice_codes: int32 [4096, 128, 128], P('ori', ('mod', 'frm')), may hold values from 0 to 2047
- pixel_mask: int32 [128, 128], P('mod'), may hold values 0 or 1
Outputs:
- log_posterior: float32 [2, 256, 4096], P('frm', 'mod', 'ori')
All inputs are finite; a program needn't handle non-finite values. No bound on the sum of `pixel_mask` on one device may be relied on, other than what follows from the above.
Results may differ from a plain program's by a relative error of at most 0.0024.
Values may be sent and summed in bfloat16 or wider, within the bound.
A program may use at most 64 MiB of HBM per device.

v0:
```python
import math

import jax
import jax.numpy as jnp
from jax import lax
from jax.sharding import PartitionSpec as P

PASSES = 8


TIME_STEP = 0.2
EDGE_SCALE = 2.0
LOG_FLOOR = -7.0
CODE_STEP = 1.0 / 256.0


def extended(x, sides, width):
    for axis, dim in sides:
        peers, length = (lax.axis_size(axis), x.shape[dim])
        up = [(i, (i + 1) % peers) for i in range(peers - 1)]
        down = [(j, i) for i, j in up]
        last = lax.slice_in_dim(x, length - width, length, axis=dim)
        leading = lax.slice_in_dim(x, 0, width, axis=dim)
        before = lax.ppermute(last, axis, up)
        after = lax.ppermute(leading, axis, down)
        x = jnp.concatenate([before, x, after], axis=dim)
    return x


def conduct(difference):
    ratio = difference / EDGE_SCALE
    return difference / (1.0 + ratio * ratio)


def relax_once(padded):
    centre = padded[:, 1:-1, :]
    column_pad = jnp.zeros((centre.shape[0], centre.shape[1], 1), jnp.float32)
    left_side = jnp.concatenate([column_pad, centre[:, :, :-1]], axis=2)
    right_side = jnp.concatenate([centre[:, :, 1:], column_pad], axis=2)
    flux_sum = conduct(padded[:, :-2, :] - centre) + conduct(padded[:, 2:, :] - centre)
    flux_sum = flux_sum + conduct(left_side - centre) + conduct(right_side - centre)
    return centre + TIME_STEP * flux_sum


def body(counts, slice_codes, pixel_mask):
    intensity = counts.astype(jnp.float32)
    module_rows = intensity.shape[1]
    total_rows = module_rows * lax.axis_size("mod")
    first_row = lax.axis_index("mod") * module_rows
    row_ids = first_row - 1 + lax.broadcasted_iota(jnp.int32, (1, module_rows + 2, 1), 1)
    inside = ((row_ids >= 0) & (row_ids < total_rows)).astype(jnp.float32)
    for pair_index in range(PASSES // 2):
        padded = extended(intensity, (("mod", 1),), 2)
        widened = relax_once(padded) * inside
        intensity = relax_once(widened)
    cleaned = intensity.astype(jnp.bfloat16) * pixel_mask.astype(jnp.bfloat16)[None]
    gathered = lax.all_gather(cleaned, "ori", axis=0, tiled=True)
    log_slices = (LOG_FLOOR + slice_codes.astype(jnp.float32) * CODE_STEP).astype(jnp.bfloat16)
    band_rows = log_slices.shape[1]
    own_mask = lax.dynamic_slice_in_dim(
        pixel_mask, lax.axis_index("frm") * band_rows, band_rows, 0
    ).astype(jnp.float32)
    local_totals = jnp.sum(jnp.exp(log_slices.astype(jnp.float32)) * own_mask[None], axis=(1, 2))
    module_totals = lax.psum(local_totals, "frm")
    product = lax.dot_general(
        gathered,
        lax.all_gather(log_slices, "frm", axis=1, tiled=True),
        (((1, 2), (1, 2)), ((), ())),
        preferred_element_type=jnp.float32,
    )
    partial_value = product - module_totals[None, :]
    scale_factor = 1.0 / math.sqrt(module_rows * lax.axis_size("mod") * intensity.shape[2])
    summed = lax.psum(partial_value, "mod")
    share_rows = summed.shape[0] // lax.axis_size("mod")
    own_rows = lax.dynamic_slice_in_dim(summed, lax.axis_index("mod") * share_rows, share_rows, 0)
    scores = own_rows * scale_factor
    peaks = lax.pmax(jnp.max(scores, axis=1), "ori")
    masses = lax.psum(jnp.sum(jnp.exp(scores - peaks[:, None]), axis=1), "ori")
    log_posterior = scores - (peaks + jnp.log(masses))[:, None]
    return log_posterior[None]


def solution(mesh):
    in_specs = (P(("frm", "ori"), "mod", None), P("ori", ("mod", "frm"), None), P("mod", None))
    out_specs = P("frm", "mod", "ori")
    return jax.shard_map(body, mesh=mesh, in_specs=in_specs, out_specs=out_specs, check_vma=False)
```

profile of v0, /device:TPU:0, one launch (start us, length us, event | category | flops | bytes accessed | tf_op | source)
XLA Modules:
  0.0 270.0 jit_solution(14299693022543329256)
XLA Ops:
  6.5 0.0 all-gather.3.cloned.1.call-start
  6.5 1.8 copy_convert_fusion.1
  8.4 5.0 %collective-permute-start = (f32[64,2,128]{2,0,1:T(8,128)S(1)}, f32[64,2,128]{2,0,1:T(8,128)S(1)}, u32[]{:S(2)}, u32[]{:S(2)}) collective-permute-start(f32[64,2,128]{2,0,1:T(8,128)S(1)} %get-tuple-element.29), channel_id=1, source_target_pairs={{0,8},{8,16},{16,24},{1,9},{9,17},{17,25},{2,10},{10,18},{18,26},{... | collective-permute-start | bytes 196616 | tf_op jit(solution)/shard_map/ppermute | solution.py:24
  13.4 1.3 collective-permute-start.1
  14.7 0.6 collective-permute-done
  15.2 4.3 %collective-permute-done.1 = f32[64,2,128]{2,0,1:T(8,128)S(1)} collective-permute-done((f32[64,2,128]{2,0,1:T(8,128)S(1)}, f32[64,2,128]{2,0,1:T(8,128)S(1)}, u32[]{:S(2)}, u32[]{:S(2)}) %collective-permute-start.1) | collective-permute-done | bytes 65568 | tf_op jit(solution)/shard_map/ppermute | solution.py:25
  19.5 0.1 pad_maximum_fusion
  19.6 0.4 fusion.10
  20.0 1.2 add_multiply_fusion.3
  21.2 0.4 fusion.14
  21.6 1.1 multiply_add_fusion.2
  22.7 3.5 %collective-permute-start.2 = (f32[64,2,128]{2,0,1:T(8,128)S(1)}, f32[64,2,128]{2,0,1:T(8,128)S(1)}, u32[]{:S(2)}, u32[]{:S(2)}) collective-permute-start(f32[64,2,128]{2,0,1:T(8,128)S(1)} %get-tuple-element.27), channel_id=1, source_target_pairs={{0,8},{8,16},{16,24},{1,9},{9,17},{17,25},{2,10},{10,18},{18,26},{... | collective-permute-start | bytes 196616 | tf_op jit(solution)/shard_map/ppermute | solution.py:24
  26.2 1.3 collective-permute-start.3
  27.5 0.6 collective-permute-done.2
  28.1 4.3 %collective-permute-done.3 = f32[64,2,128]{2,0,1:T(8,128)S(1)} collective-permute-done((f32[64,2,128]{2,0,1:T(8,128)S(1)}, f32[64,2,128]{2,0,1:T(8,128)S(1)}, u32[]{:S(2)}, u32[]{:S(2)}) %collective-permute-start.3) | collective-permute-done | bytes 65568 | tf_op jit(solution)/shard_map/ppermute | solution.py:25
  32.4 0.1 pad_maximum_fusion.1
  32.5 0.4 fusion.9
  32.9 1.2 add_multiply_fusion.2
  34.2 0.4 fusion.13
  34.5 1.1 multiply_add_fusion.1
  35.6 3.5 %collective-permute-start.4 = (f32[64,2,128]{2,0,1:T(8,128)S(1)}, f32[64,2,128]{2,0,1:T(8,128)S(1)}, u32[]{:S(2)}, u32[]{:S(2)}) collective-permute-start(f32[64,2,128]{2,0,1:T(8,128)S(1)} %get-tuple-element.25), channel_id=1, source_target_pairs={{0,8},{8,16},{16,24},{1,9},{9,17},{17,25},{2,10},{10,18},{18,26},{... | collective-permute-start | bytes 196616 | tf_op jit(solution)/shard_map/ppermute | solution.py:24
  39.1 1.3 collective-permute-start.5
  40.4 0.6 collective-permute-done.4
  41.0 4.3 %collective-permute-done.5 = f32[64,2,128]{2,0,1:T(8,128)S(1)} collective-permute-done((f32[64,2,128]{2,0,1:T(8,128)S(1)}, f32[64,2,128]{2,0,1:T(8,128)S(1)}, u32[]{:S(2)}, u32[]{:S(2)}) %collective-permute-start.5) | collective-permute-done | bytes 65568 | tf_op jit(solution)/shard_map/ppermute | solution.py:25
  45.3 0.1 pad_maximum_fusion.2
  45.4 0.4 fusion.8
  45.8 1.2 add_multiply_fusion.1
  47.1 0.4 fusion.12
  47.4 0.0 copy-start
  47.4 1.1 multiply_add_fusion
  48.6 1.9 collective-permute-start.6
  50.5 1.5 collective-permute-start.7
  52.0 0.0 copy-done
  52.0 0.4 collective-permute-done.6
  52.4 4.3 %collective-permute-done.7 = f32[64,2,128]{2,0,1:T(8,128)S(1)} collective-permute-done((f32[64,2,128]{2,0,1:T(8,128)S(1)}, f32[64,2,128]{2,0,1:T(8,128)S(1)}, u32[]{:S(2)}, u32[]{:S(2)}) %collective-permute-start.7) | collective-permute-done | bytes 65568 | tf_op jit(solution)/shard_map/ppermute | solution.py:25
  56.6 0.1 pad_maximum_fusion.3
  56.7 0.4 fusion.7
  57.1 1.2 add_multiply_fusion
  58.4 0.4 fusion.11
  58.7 2.0 fusion.4
  60.7 0.0 all-gather.3.cloned.1.call-update
  60.7 0.0 all-gather.5.cloned.1.call-start
  60.8 7.8 %multiply_reduce_fusion = (f32[1024]{0:T(1024)S(1)}, bf16[1024,16,128]{2,0,1:T(8,128)(2,1)}) fusion(f32[16,128]{1,0:T(8,128)S(1)} %dynamic-slice_convert_fusion, s32[1024,16,128]{2,1,0:T(8,128)} %param.4), kind=kLoop, calls=%fused_computation.4 | loop fusion | flops 14679040 | bytes 12595200 | tf_op jit(solution)/shard_map/reduce_sum | solution.py:63
  68.6 0.0 all-gather.5.cloned.1.call-update
  68.6 0.0 all-reduce.18.cloned.1.call-start
  68.6 4.9 %psum.21 = f32[1024]{0:T(1024)S(1)} all-reduce(f32[1024]{0:T(1024)S(1)} %get-tuple-element.5), channel_id=1, replica_groups=mesh['mod'=4,'frm'=2,'ori'=4] {'frm'}, use_global_device_ids=true, to_apply=%region_1.0 | all-reduce | flops 1024 | bytes 8192 | tf_op jit(solution)/shard_map/psum | solution.py:64
  73.6 8.1 %all-gather.3.cloned.1.call-done = bf16[256,32,128]{2,0,1:T(8,128)(2,1)} async-done(((bf16[64,32,128]{2,0,1:T(8,128)(2,1)}), bf16[256,32,128]{2,0,1:T(8,128)(2,1)}) %all-gather.3.cloned.1.call-update) | async-done | bytes 2097168 | tf_op jit(solution)/shard_map/all_gather | solution.py:57
  81.7 105.5 %all-gather.5.cloned.1.call-done = bf16[1024,32,128]{2,0,1:T(8,128)(2,1)} async-done(((bf16[1024,16,128]{2,0,1:T(8,128)(2,1)}), bf16[1024,32,128]{2,0,1:T(8,128)(2,1)}) %all-gather.5.cloned.1.call-update) | async-done | bytes 8388624 | tf_op jit(solution)/shard_map/all_gather | solution.py:67
  187.2 7.4 %fusion.3 = f32[256,1024]{1,0:T(8,128)} fusion(bf16[256,32,128]{2,0,1:T(8,128)(2,1)} %all-gather.3.cloned.1.call-done, bf16[1024,32,128]{2,0,1:T(8,128)(2,1)} %all-gather.5.cloned.1.call-done, f32[1024]{0:T(1024)S(1)} %psum.21), kind=kOutput, calls=%fused_computation.6 | convolution fusion | flops 2147745792 | bytes 11538432 | tf_op jit(solution)/shard_map/dot_general | solution.py:65
  194.7 0.0 all-reduce.18.cloned.1.call-update
  194.7 52.1 %all-reduce.18.cloned.1.call-done = f32[256,1024]{1,0:T(8,128)} async-done(((f32[256,1024]{1,0:T(8,128)}), f32[256,1024]{1,0:T(8,128)}) %all-reduce.18.cloned.1.call-update) | async-done | bytes 1048592 | tf_op jit(solution)/shard_map/psum | solution.py:73
  246.7 1.1 fusion.5
  247.8 6.9 %pmax.7 = f32[64]{0:T(128)S(1)} all-reduce(f32[64]{0:T(128)S(1)} %fusion.5), channel_id=1, replica_groups=mesh['mod'=4,'frm'=2,'ori'=4] {'ori'}, use_global_device_ids=true, to_apply=%region_4.0 | all-reduce | flops 64 | bytes 512 | tf_op jit(solution)/shard_map/pmax | solution.py:77
  254.7 1.2 exponential_reduce_fusion
  255.8 5.9 %psum.23 = f32[64]{0:T(128)S(1)} all-reduce(f32[64]{0:T(128)S(1)} %exponential_reduce_fusion), channel_id=1, replica_groups=mesh['mod'=4,'frm'=2,'ori'=4] {'ori'}, use_global_device_ids=true, to_apply=%region_6.0 | all-reduce | flops 64 | bytes 512 | tf_op jit(solution)/shard_map/psum | solution.py:78
  261.8 1.7 subtract_bitcast_fusion
  (8 shorter events, 0.1 us)
Async XLA Ops:
  6.5 75.1 %all-gather.3.cloned.1.call-start = ((), (), s32[]{:S(2)}) async-start(), calls=%async_computation | async-start | bytes 2621440 | tf_op jit(solution)/shard_map/all_gather | solution.py:57
  8.4 6.9 %collective-permute-start = (f32[64,2,128]{2,0,1:T(8,128)S(1)}, f32[64,2,128]{2,0,1:T(8,128)S(1)}, u32[]{:S(2)}, u32[]{:S(2)}) collective-permute-start(f32[64,2,128]{2,0,1:T(8,128)S(1)} %get-tuple-element.29), channel_id=1, source_target_pairs={{0,8},{8,16},{16,24},{1,9},{9,17},{17,25},{2,10},{10,18},{18,26},{... | collective-permute-start | bytes 196616 | tf_op jit(solution)/shard_map/ppermute | solution.py:24
  13.4 6.2 %collective-permute-start.1 = (f32[64,2,128]{2,0,1:T(8,128)S(1)}, f32[64,2,128]{2,0,1:T(8,128)S(1)}, u32[]{:S(2)}, u32[]{:S(2)}) collective-permute-start(f32[64,2,128]{2,0,1:T(8,128)S(1)} %get-tuple-element.30), channel_id=1, source_target_pairs={{8,0},{16,8},{24,16},{9,1},{17,9},{25,17},{10,2},{18,10},{26,18},{... | collective-permute-start | bytes 196616 | tf_op jit(solution)/shard_map/ppermute | solution.py:25
  22.7 5.4 %collective-permute-start.2 = (f32[64,2,128]{2,0,1:T(8,128)S(1)}, f32[64,2,128]{2,0,1:T(8,128)S(1)}, u32[]{:S(2)}, u32[]{:S(2)}) collective-permute-start(f32[64,2,128]{2,0,1:T(8,128)S(1)} %get-tuple-element.27), channel_id=1, source_target_pairs={{0,8},{8,16},{16,24},{1,9},{9,17},{17,25},{2,10},{10,18},{18,26},{... | collective-permute-start | bytes 196616 | tf_op jit(solution)/shard_map/ppermute | solution.py:24
  26.2 6.2 %collective-permute-start.3 = (f32[64,2,128]{2,0,1:T(8,128)S(1)}, f32[64,2,128]{2,0,1:T(8,128)S(1)}, u32[]{:S(2)}, u32[]{:S(2)}) collective-permute-start(f32[64,2,128]{2,0,1:T(8,128)S(1)} %get-tuple-element.28), channel_id=1, source_target_pairs={{8,0},{16,8},{24,16},{9,1},{17,9},{25,17},{10,2},{18,10},{26,18},{... | collective-permute-start | bytes 196616 | tf_op jit(solution)/shard_map/ppermute | solution.py:25
  35.6 5.4 %collective-permute-start.4 = (f32[64,2,128]{2,0,1:T(8,128)S(1)}, f32[64,2,128]{2,0,1:T(8,128)S(1)}, u32[]{:S(2)}, u32[]{:S(2)}) collective-permute-start(f32[64,2,128]{2,0,1:T(8,128)S(1)} %get-tuple-element.25), channel_id=1, source_target_pairs={{0,8},{8,16},{16,24},{1,9},{9,17},{17,25},{2,10},{10,18},{18,26},{... | collective-permute-start | bytes 196616 | tf_op jit(solution)/shard_map/ppermute | solution.py:24
  39.1 6.2 %collective-permute-start.5 = (f32[64,2,128]{2,0,1:T(8,128)S(1)}, f32[64,2,128]{2,0,1:T(8,128)S(1)}, u32[]{:S(2)}, u32[]{:S(2)}) collective-permute-start(f32[64,2,128]{2,0,1:T(8,128)S(1)} %get-tuple-element.26), channel_id=1, source_target_pairs={{8,0},{16,8},{24,16},{9,1},{17,9},{25,17},{10,2},{18,10},{26,18},{... | collective-permute-start | bytes 196616 | tf_op jit(solution)/shard_map/ppermute | solution.py:25
  47.4 4.5 %copy-start = (s32[32,128]{1,0:T(8,128)S(1)}, s32[32,128]{1,0:T(8,128)}, u32[]{:S(2)}) copy-start(s32[32,128]{1,0:T(8,128)} %param.5) | copy-start | bytes 49156
  48.6 3.8 %collective-permute-start.6 = (f32[64,2,128]{2,0,1:T(8,128)S(1)}, f32[64,2,128]{2,0,1:T(8,128)S(1)}, u32[]{:S(2)}, u32[]{:S(2)}) collective-permute-start(f32[64,2,128]{2,0,1:T(8,128)S(1)} %get-tuple-element.23), channel_id=1, source_target_pairs={{0,8},{8,16},{16,24},{1,9},{9,17},{17,25},{2,10},{10,18},{18,26},{... | collective-permute-start | bytes 196616 | tf_op jit(solution)/shard_map/ppermute | solution.py:24
  50.5 6.2 %collective-permute-start.7 = (f32[64,2,128]{2,0,1:T(8,128)S(1)}, f32[64,2,128]{2,0,1:T(8,128)S(1)}, u32[]{:S(2)}, u32[]{:S(2)}) collective-permute-start(f32[64,2,128]{2,0,1:T(8,128)S(1)} %get-tuple-element.24), channel_id=1, source_target_pairs={{8,0},{16,8},{24,16},{9,1},{17,9},{25,17},{10,2},{18,10},{26,18},{... | collective-permute-start | bytes 196616 | tf_op jit(solution)/shard_map/ppermute | solution.py:25
  60.7 126.5 %all-gather.5.cloned.1.call-start = ((), (), s32[]{:S(2)}) async-start(), calls=%async_computation.1 | async-start | bytes 12582912 | tf_op jit(solution)/shard_map/all_gather | solution.py:67
  68.6 178.1 %all-reduce.18.cloned.1.call-start = ((), (), s32[]{:S(2)}) async-start(), calls=%async_computation.2 | async-start | bytes 2097152 | tf_op jit(solution)/shard_map/psum | solution.py:73
Sparse Core Ops, SparseCore 0:
  60.9 20.7 all-gather.2
  83.2 103.9 all-gather.4
  194.8 51.8 all-reduce.17
where the time goes:
time: 271 us; the launch traced here: 270 us
  waiting for transfers between devices  185 us (68%)
  other arithmetic  24.2 us (9%)
  starting transfers between devices  19.3 us (7%)
  blocking collectives  17.7 us (7%)
  between operations  13.4 us (5%)
  matrix products  7.45 us (3%)
  local copies, waits for them, and re-layouts  3.11 us (1%)
    all_gather x1, waiting for transfers between devices, body(): lax.all_gather(log_slices, 'frm', axis=1, tiled=True)  106 us
    psum x1, waiting for transfers between devices, body(): summed = lax.psum(partial_value, 'mod')  52.1 us
    ppermute x4, waiting for transfers between devices, extended(): after = lax.ppermute(leading, axis, down)  17.1 us
    ppermute x4, starting transfers between devices, extended(): before = lax.ppermute(last, axis, up)  13.8 us
    all_gather x1, waiting for transfers between devices, body(): gathered = lax.all_gather(cleaned, 'ori', axis=0, tiled=True)  8.08 us
    reduce_sum x1, other arithmetic, body(): jnp.sum(jnp.exp(log_slices.astype(jnp.float32)) * own_mask[None], axis=(1...  7.77 us
    dot_general x1, matrix products, body(): lax.dot_general(gathered, lax.all_gather(log_slices, 'frm', axis=1, tiled...  7.45 us
    pmax x1, blocking collectives, body(): peaks = lax.pmax(jnp.max(scores, axis=1), 'ori')  6.85 us
  transfers between devices with their start and end apart: 11, of which 11 were waited for; matrix products, arithmetic and copies ran while one was open for 3% of the time, Pallas kernels for 0%

commit v1 on v0

v1 whole, which is shorter than its diff:
```python
import functools
import math

import jax
import jax.numpy as jnp
from jax import lax
from jax.experimental import pallas as pl
from jax.experimental.pallas import tpu as pltpu
from jax.sharding import PartitionSpec as P

PASSES = 8
TIME_STEP = 0.2
EDGE_SCALE = 2.0
LOG_FLOOR = -7.0
CODE_STEP = 1.0 / 256.0
GROUPS = 2
SLICE_CHUNK = 128
MESH = pl.DeviceIdType.MESH


def conduct(d):
    ratio = d * (1.0 / EDGE_SCALE)
    return d / (1.0 + ratio * ratio)


def conduct_pair(a, b):
    ra = a * (1.0 / EDGE_SCALE)
    rb = b * (1.0 / EDGE_SCALE)
    da = 1.0 + ra * ra
    db = 1.0 + rb * rb
    return (a * db + b * da) / (da * db)


def flip(h, b):
    return h + b - 2 * b * lax.rem(h // b, 2)


def kernel(
    dims, counts, codes, mask, out,
    codes_v, logs, inten, halo_s, halo_r, band_s, frames, cross, xrecv, zrecv,
    stat_s, stat_r, totals,
    code_sem, hs_sem, hr_sem, own_sem, gs_sem, gr_sem, xs_sem, xr_sem, zs_sem, zr_sem,
    ts_sem, tr_sem,
):
    nm, nf, no, fr, rows, orient, band = dims
    m, f, o = lax.axis_index("mod"), lax.axis_index("frm"), lax.axis_index("ori")
    sizes = {"mod": (m, nm), "frm": (f, nf), "ori": (o, no)}
    lanes = counts.shape[1]
    depth = band * lanes
    high = rows + 2 * PASSES
    gsz = fr // GROUPS
    group = no * fr
    share = group // nm
    chunks = orient // SLICE_CHUNK

    def other(axis, d):
        me, n = sizes[axis]
        return lax.rem(me + d, n)

    def code_copy(c):
        span = SLICE_CHUNK * band
        at = pl.ds(c * span, span)
        return pltpu.make_async_copy(codes.at[at], codes_v.at[at], code_sem.at[c])

    for c in range(chunks):
        code_copy(c).start()

    barrier = pltpu.get_barrier_semaphore()
    for axis in ("mod", "frm", "ori"):
        for d in range(1, sizes[axis][1]):
            pl.semaphore_signal(
                barrier, inc=1, device_id={axis: other(axis, d)}, device_id_type=MESH
            )

    def load_row(i, carry):
        inten[PASSES + i] = counts[pl.ds(i, fr, stride=rows), :].astype(jnp.float32)
        return carry

    lax.fori_loop(0, rows, load_row, 0)
    for i in range(PASSES):
        halo_s[0, i] = inten[PASSES + i].astype(jnp.bfloat16)
        halo_s[1, i] = inten[rows + i].astype(jnp.bfloat16)
    pl.semaphore_wait(barrier, nm + nf + no - 3)

    def halo_copy(side):
        return pltpu.make_async_remote_copy(
            src_ref=halo_s.at[side],
            dst_ref=halo_r.at[1 - side],
            send_sem=hs_sem.at[side],
            recv_sem=hr_sem.at[1 - side],
            device_id={"mod": other("mod", nm - 1 if side == 0 else 1)},
            device_id_type=MESH,
        )

    first, last = m == 0, m == nm - 1

    @pl.when(jnp.logical_not(first))
    def _():
        halo_copy(0).start()

    @pl.when(jnp.logical_not(last))
    def _():
        halo_copy(1).start()

    def slice_chunk(c):
        code_copy(c).wait()
        base = c * (SLICE_CHUNK * band)
        acc = jnp.zeros((SLICE_CHUNK, lanes), jnp.float32)
        for s in range(band):
            raw = codes_v[pl.ds(base + s, SLICE_CHUNK, stride=band), :]
            value = (LOG_FLOOR + raw.astype(jnp.float32) * CODE_STEP).astype(jnp.bfloat16)
            logs[pl.ds(c * SLICE_CHUNK, SLICE_CHUNK), pl.ds(s * lanes, lanes)] = value
            weight = mask[pl.ds(f * band + s, 1), :].astype(jnp.float32)
            acc = acc + jnp.exp(value.astype(jnp.float32)) * weight
        totals[:, pl.ds(c * SLICE_CHUNK, SLICE_CHUNK)] = jnp.sum(acc.T, axis=0, keepdims=True)

    early = chunks // 2
    for c in range(early):
        slice_chunk(c)

    @pl.when(first)
    def _():
        inten[pl.ds(0, PASSES)] = jnp.zeros((PASSES, fr, lanes), jnp.float32)

    @pl.when(jnp.logical_not(first))
    def _():
        halo_copy(1).wait_recv()
        inten[pl.ds(0, PASSES)] = halo_r[0].astype(jnp.float32)
        halo_copy(0).wait_send()

    @pl.when(last)
    def _():
        inten[pl.ds(PASSES + rows, PASSES)] = jnp.zeros((PASSES, fr, lanes), jnp.float32)

    @pl.when(jnp.logical_not(last))
    def _():
        halo_copy(0).wait_recv()
        inten[pl.ds(PASSES + rows, PASSES)] = halo_r[1].astype(jnp.float32)
        halo_copy(1).wait_send()

    lane = lax.broadcasted_iota(jnp.int32, (gsz, lanes), 1)
    at_left, at_right = lane == 0, lane == lanes - 1
    row_min = jnp.where(first, PASSES, 0)
    row_max = jnp.where(last, PASSES + rows, high)

    def diffuse(g):
        part = pl.ds(g * gsz, gsz)

        def one_row(i, c, before):
            below = inten[i + 1, part, :]
            after = conduct(below - c)
            left = jnp.where(at_left, 0.0, pltpu.roll(c, 1, 1))
            right = jnp.where(at_right, 0.0, pltpu.roll(c, lanes - 1, 1))
            side = conduct_pair(left - c, right - c)
            step = jnp.where(jnp.logical_and(i >= row_min, i < row_max), TIME_STEP, 0.0)
            inten[i, part, :] = c + step * ((after - before) + side)
            return below, after

        def one_pass(p, carry):
            centre = inten[p + 1, part, :]
            before = conduct(centre - inten[p, part, :])

            def two_rows(k, state):
                i = p + 1 + 2 * k
                c, b = one_row(i, *state)
                return one_row(i + 1, c, b)

            lax.fori_loop(0, high // 2 - 1 - p, two_rows, (centre, before))
            return carry

        lax.fori_loop(0, PASSES, one_pass, 0)
        for i in range(rows):
            good = mask[i : i + 1, :].astype(jnp.float32)
            band_s[
                pl.ds((i // band) * fr + g * gsz, gsz), pl.ds((i % band) * lanes, lanes)
            ] = (inten[PASSES + i, part, :] * good).astype(jnp.bfloat16)

    def slot(ff, oo, g):
        return frames.at[pl.ds((ff * no + oo) * fr + g * gsz, gsz)]

    pending = []
    count = [0]

    def arrived(ff, oo, g):
        pltpu.make_async_remote_copy(
            src_ref=slot(ff, oo, g), dst_ref=slot(ff, oo, g),
            send_sem=gs_sem.at[0], recv_sem=gr_sem.at[ff * no + oo, g],
            device_id={"ori": other("ori", 1)}, device_id_type=MESH,
        ).wait_recv()

    def send(src, ff, oo, g, target):
        copy = pltpu.make_async_remote_copy(
            src_ref=src, dst_ref=slot(ff, oo, g),
            send_sem=gs_sem.at[count[0]], recv_sem=gr_sem.at[ff * no + oo, g],
            device_id=target, device_id_type=MESH,
        )
        count[0] += 1
        copy.start()
        pending.append(copy)

    def banded(ff, g):
        return band_s.at[pl.ds(ff * fr + g * gsz, gsz)]

    bits = []
    b = no // 2
    while b >= 1:
        bits.append(b)
        b //= 2

    own_copies = []
    for g in range(GROUPS):
        diffuse(g)
        for d in range(1, nf):
            fd = other("frm", d)
            send(banded(fd, g), f, o, g, {"frm": fd})
        own = pltpu.make_async_copy(banded(f, g), slot(f, o, g), own_sem.at[g])
        own.start()
        own_copies.append(own)
        send(banded(f, g), f, o, g, {"ori": flip(o, bits[0])})

    todo = list(range(early, chunks))

    def some_slices(n):
        for _ in range(min(n, len(todo))):
            slice_chunk(todo.pop(0))

    for g in range(GROUPS):
        for d in range(1, nf):
            fd = other("frm", d)
            arrived(fd, o, g)
            send(slot(fd, o, g), fd, o, g, {"ori": flip(o, bits[0])})
        some_slices(1)
    some_slices(chunks)
    for own in own_copies:
        own.wait()
    held = [o]
    for k, b in enumerate(bits):
        gained = [flip(h, b) for h in held]
        if k > 0:
            for g in range(GROUPS):
                for d in range(nf):
                    for h in held:
                        send(slot(other("frm", d), h, g), other("frm", d), h, g, {"ori": flip(o, b)})
        nxt = bits[k + 1] if k + 1 < len(bits) else None
        for d in range(nf):
            for g in range(GROUPS):
                for h in gained:
                    arrived(other("frm", d), h, g)
        held = held + gained

    tile = 256
    order = [(nm // 2 + j) % nm for j in range(nm)]
    order = [q for q in order if q != 0] + [0]

    def multiply(ff):
        start = pl.multiple_of(ff * group, group)

        def one_tile(t, carry):
            at = pl.multiple_of(t * tile, tile)
            cross[pl.ds(start, group), pl.ds(at, tile)] = (
                lax.dot_general(
                    frames[pl.ds(start, group), :],
                    logs[pl.ds(at, tile), :],
                    (((1,), (1,)), ((), ())),
                    preferred_element_type=jnp.float32,
                )
                - totals[:, pl.ds(at, tile)]
            )
            return carry

        lax.fori_loop(0, orient // tile, one_tile, 0)

    def part_of(ref, ff, mm):
        return ref.at[pl.ds(ff * group + mm * share, share)]

    def x_copy(src_f, dst_f, mm, n):
        return pltpu.make_async_remote_copy(
            src_ref=part_of(cross, dst_f, mm), dst_ref=part_of(xrecv, src_f, mm),
            send_sem=xs_sem.at[n], recv_sem=xr_sem.at[src_f, mm],
            device_id={"frm": dst_f}, device_id_type=MESH,
        )

    n = 0
    for d in range(1, nf):
        fd = other("frm", d)
        multiply(fd)
        for q in order:
            copy = x_copy(f, fd, other("mod", q), n)
            copy.start()
            pending.append(copy)
            n += 1
    multiply(f)

    def z_copy(src_m, dst_m, n):
        return pltpu.make_async_remote_copy(
            src_ref=part_of(cross, f, dst_m), dst_ref=zrecv.at[src_m],
            send_sem=zs_sem.at[n], recv_sem=zr_sem.at[src_m],
            device_id={"mod": dst_m}, device_id_type=MESH,
        )

    score = None
    for k, q in enumerate(order):
        mm = other("mod", q)
        at = pl.ds(pl.multiple_of(f * group + mm * share, share), share)
        value = cross[at, :]
        for d in range(1, nf):
            fd = other("frm", d)
            x_copy(fd, other("frm", 1), mm, 0).wait_recv()
            value = value + xrecv[pl.ds(pl.multiple_of(fd * group + mm * share, share), share), :]
        if q == 0:
            score = value
        else:
            cross[at, :] = value
            copy = z_copy(m, mm, k)
            copy.start()
            pending.append(copy)
    for q in order[:-1]:
        mm = other("mod", q)
        z_copy(mm, mm, 0).wait_recv()
        score = score + zrecv[mm]
    score = score * (1.0 / math.sqrt(rows * nm * lanes))
    peak = jnp.max(score, axis=1, keepdims=True)
    mass = jnp.sum(jnp.exp(score - peak), axis=1, keepdims=True)
    wide = lax.broadcasted_iota(jnp.int32, (share, 128), 1)
    stat_s[...] = jnp.where(wide < 64, peak, mass)

    def t_copy(src_o, dst_o, n):
        return pltpu.make_async_remote_copy(
            src_ref=stat_s, dst_ref=stat_r.at[src_o],
            send_sem=ts_sem.at[n], recv_sem=tr_sem.at[src_o],
            device_id={"ori": dst_o}, device_id_type=MESH,
        )

    for d in range(1, no):
        copy = t_copy(o, other("ori", d), d)
        copy.start()
        pending.append(copy)
    peaks, masses = [peak], [mass]
    for d in range(1, no):
        od = other("ori", d)
        t_copy(od, od, 0).wait_recv()
        got = stat_r[od]
        peaks.append(got[:, 0:1])
        masses.append(got[:, 64:65])
    top = functools.reduce(jnp.maximum, peaks)
    weight = sum(s * jnp.exp(p - top) for p, s in zip(peaks, masses))
    out[...] = score - (top + jnp.log(weight))
    for copy in pending:
        copy.wait_send()


def body(counts, slice_codes, pixel_mask):
    nm, nf, no = (lax.axis_size(a) for a in ("mod", "frm", "ori"))
    fr, rows, lanes = counts.shape
    orient, band, _ = slice_codes.shape
    group = no * fr
    share = group // nm
    depth = band * lanes
    high = rows + 2 * PASSES
    dims = (nm, nf, no, fr, rows, orient, band)
    dma = pltpu.SemaphoreType.DMA
    f32, bf16 = jnp.float32, jnp.bfloat16
    vmem = pl.BlockSpec(memory_space=pltpu.VMEM)
    result = pl.pallas_call(
        functools.partial(kernel, dims),
        out_shape=jax.ShapeDtypeStruct((share, orient), f32),
        in_specs=[vmem, pl.BlockSpec(memory_space=pl.ANY), vmem],
        out_specs=vmem,
        scratch_shapes=[
            pltpu.VMEM((orient * band, lanes), jnp.int32),
            pltpu.VMEM((orient, depth), bf16),
            pltpu.VMEM((high, fr, lanes), f32),
            pltpu.VMEM((2, PASSES, fr, lanes), bf16),
            pltpu.VMEM((2, PASSES, fr, lanes), bf16),
            pltpu.VMEM((nf * fr, depth), bf16),
            pltpu.VMEM((nf * group, depth), bf16),
            pltpu.VMEM((nf * group, orient), f32),
            pltpu.VMEM((nf * group, orient), f32),
            pltpu.VMEM((nm, share, orient), f32),
            pltpu.VMEM((share, 128), f32),
            pltpu.VMEM((no, share, 128), f32),
            pltpu.VMEM((1, orient), f32),
            dma((orient // SLICE_CHUNK,)),
            dma((2,)),
            dma((2,)),
            dma((GROUPS,)),
            dma((GROUPS * nf * (no + 1),)),
            dma((nf * no, GROUPS)),
            dma((nf * nm,)),
            dma((nf, nm)),
            dma((nm,)),
            dma((nm,)),
            dma((no,)),
            dma((no,)),
        ],
        compiler_params=pltpu.CompilerParams(collective_id=0, has_side_effects=True),
    )(counts.reshape(fr * rows, lanes), slice_codes.reshape(orient * band, lanes), pixel_mask)
    return result[None]


def solution(mesh):
    in_specs = (P(("frm", "ori"), "mod", None), P("ori", ("mod", "frm"), None), P("mod", None))
    out_specs = P("frm", "mod", "ori")
    return jax.shard_map(body, mesh=mesh, in_specs=in_specs, out_specs=out_specs, check_vma=False)
```

time: 271 us -> 93.2 us (0.34)
  waiting for transfers between devices: 185 us -> 0 us
  Pallas kernels: 0 us -> 90.8 us
  other arithmetic: 24.2 us -> 0 us
  starting transfers between devices: 19.3 us -> 0 us
  blocking collectives: 17.7 us -> 0 us
  between operations: 13.4 us -> 0.01 us
  matrix products: 7.45 us -> 0 us
    all_gather x2 -> x0, waiting for transfers between devices: 114 us -> none  [the longest x1 106 us: body(): lax.all_gather(log_slices, 'frm', axis=1, tiled=True)]
    pallas_call x0 -> x1, Pallas kernels: none -> 90.8 us  [body(): pl.pallas_call(functools.partial(kernel, dims), out_shape=jax.ShapeDtypeS...]
    psum x1 -> x0, waiting for transfers between devices: 52.1 us -> none  [body(): summed = lax.psum(partial_value, 'mod')]
    ppermute x8 -> x0, waiting for transfers between devices: 19.2 us -> none  [the longest x4 17.1 us: extended(): after = lax.ppermute(leading, axis, down)]
    ppermute x8 -> x0, starting transfers between devices: 19.2 us -> none  [the longest x4 13.8 us: extended(): before = lax.ppermute(last, axis, up)]
    psum x2 -> x0, blocking collectives: 10.9 us -> none  [the longest x1 5.92 us: body(): masses = lax.psum(jnp.sum(jnp.exp(scores - peaks[:, None]), axis=1), 'ori')]
    reduce_sum x2 -> x0, other arithmetic: 8.93 us -> none  [the longest x1 7.77 us: body(): jnp.sum(jnp.exp(log_slices.astype(jnp.float32)) * own_mask[None], axis=(1...]
    dot_general x1 -> x0, matrix products: 7.45 us -> none  [body(): lax.dot_general(gathered, lax.all_gather(log_slices, 'frm', axis=1, tiled...]
  transfers between devices with their start and end apart: 11 -> 0, of which waited for: 11 -> 0; matrix products, arithmetic and copies ran while one was open for 3% -> 0% of each run, Pallas kernels for 0% -> 0%
where the time goes in v1:
time: 93.2 us; the launch traced here: 92.4 us
  Pallas kernels  90.8 us (97%)
  local copies, waits for them, and re-layouts  1.67 us (2%)
    pallas_call x1, Pallas kernels, body(): pl.pallas_call(functools.partial(kernel, dims), out_shape=jax.ShapeDtypeS...  90.8 us

profile of v1, /device:TPU:0, one launch (start us, length us, event | category | flops | bytes accessed | tf_op | source)
XLA Modules:
  0.0 92.4 jit_solution(16457238809893010419)
XLA Ops:
  0.0 90.8 %shard_map.37 = f32[64,1024]{1,0:T(8,128)} custom-call(s32[2048,128]{1,0:T(8,128)} %bitcast.4, s32[16384,128]{1,0:T(8,128)} %bitcast.3, s32[32,128]{1,0:T(8,128)} %mask.1), custom_call_target="tpu_custom_call" | custom-call | tf_op jit(solution)/shard_map/pallas_call | solution.py:364
  90.8 1.7 %copy.5 = f32[1,64,1024]{2,1,0:T(8,128)} copy(f32[1,64,1024]{2,1,0:T(8,128)} %bitcast.5) | data formatting | bytes 524288

commit v2 on v1

--- a/solution.py
+++ b/solution.py
@@ -13,22 +13,21 @@
 EDGE_SCALE = 2.0
 LOG_FLOOR = -7.0
 CODE_STEP = 1.0 / 256.0
-GROUPS = 2
+GROUPS = 4
+STRIDE_ROWS = 8
 SLICE_CHUNK = 128
 MESH = pl.DeviceIdType.MESH
 
 
+SQUARE = EDGE_SCALE * EDGE_SCALE
+
+
 def conduct(d):
-    ratio = d * (1.0 / EDGE_SCALE)
-    return d / (1.0 + ratio * ratio)
+    return d / (SQUARE + d * d)
 
 
 def conduct_pair(a, b):
-    ra = a * (1.0 / EDGE_SCALE)
-    rb = b * (1.0 / EDGE_SCALE)
-    da = 1.0 + ra * ra
-    db = 1.0 + rb * rb
-    return (a * db + b * da) / (da * db)
+    return (a + b) * (SQUARE + a * b) / ((SQUARE + a * a) * (SQUARE + b * b))
 
 
 def flip(h, b):
@@ -77,6 +76,7 @@
         return carry
 
     lax.fori_loop(0, rows, load_row, 0)
+    inten[pl.ds(high, STRIDE_ROWS)] = jnp.zeros((STRIDE_ROWS, fr, lanes), jnp.float32)
     for i in range(PASSES):
         halo_s[0, i] = inten[PASSES + i].astype(jnp.bfloat16)
         halo_s[1, i] = inten[rows + i].astype(jnp.bfloat16)
@@ -146,26 +146,30 @@
     def diffuse(g):
         part = pl.ds(g * gsz, gsz)
 
-        def one_row(i, c, before):
-            below = inten[i + 1, part, :]
-            after = conduct(below - c)
-            left = jnp.where(at_left, 0.0, pltpu.roll(c, 1, 1))
-            right = jnp.where(at_right, 0.0, pltpu.roll(c, lanes - 1, 1))
-            side = conduct_pair(left - c, right - c)
-            step = jnp.where(jnp.logical_and(i >= row_min, i < row_max), TIME_STEP, 0.0)
-            inten[i, part, :] = c + step * ((after - before) + side)
-            return below, after
-
         def one_pass(p, carry):
             centre = inten[p + 1, part, :]
             before = conduct(centre - inten[p, part, :])
 
-            def two_rows(k, state):
-                i = p + 1 + 2 * k
-                c, b = one_row(i, *state)
-                return one_row(i + 1, c, b)
-
-            lax.fori_loop(0, high // 2 - 1 - p, two_rows, (centre, before))
+            def some_rows(k, state):
+                c, before = state
+                i = p + 1 + STRIDE_ROWS * k
+                below = [inten[i + r + 1, part, :] for r in range(STRIDE_ROWS)]
+                fresh = []
+                for r in range(STRIDE_ROWS):
+                    after = conduct(below[r] - c)
+                    left = jnp.where(at_left, 0.0, pltpu.roll(c, 1, 1))
+                    right = jnp.where(at_right, 0.0, pltpu.roll(c, lanes - 1, 1))
+                    side = conduct_pair(left - c, right - c)
+                    inside = jnp.logical_and(i + r >= row_min, i + r < row_max)
+                    step = jnp.where(inside, TIME_STEP * SQUARE, 0.0)
+                    fresh.append(c + step * ((after - before) + side))
+                    c, before = below[r], after
+                for r in range(STRIDE_ROWS):
+                    inten[i + r, part, :] = fresh[r]
+                return c, before
+
+            trips = (high - 2 * p - 3 + STRIDE_ROWS) // STRIDE_ROWS
+            lax.fori_loop(0, trips, some_rows, (centre, before))
             return carry
 
         lax.fori_loop(0, PASSES, one_pass, 0)
@@ -207,50 +211,65 @@
         bits.append(b)
         b //= 2
 
-    own_copies = []
-    for g in range(GROUPS):
-        diffuse(g)
+    held = [[o]]
+    for b in bits:
+        held.append(held[-1] + [flip(h, b) for h in held[-1]])
+
+    def first_hop(g):
         for d in range(1, nf):
             fd = other("frm", d)
             send(banded(fd, g), f, o, g, {"frm": fd})
         own = pltpu.make_async_copy(banded(f, g), slot(f, o, g), own_sem.at[g])
         own.start()
-        own_copies.append(own)
         send(banded(f, g), f, o, g, {"ori": flip(o, bits[0])})
-
-    todo = list(range(early, chunks))
-
-    def some_slices(n):
-        for _ in range(min(n, len(todo))):
-            slice_chunk(todo.pop(0))
-
-    for g in range(GROUPS):
+        own.wait()
+
+    def second_hop(g):
         for d in range(1, nf):
             fd = other("frm", d)
             arrived(fd, o, g)
             send(slot(fd, o, g), fd, o, g, {"ori": flip(o, bits[0])})
-        some_slices(1)
-    some_slices(chunks)
-    for own in own_copies:
-        own.wait()
-    held = [o]
-    for k, b in enumerate(bits):
-        gained = [flip(h, b) for h in held]
-        if k > 0:
-            for g in range(GROUPS):
-                for d in range(nf):
-                    for h in held:
-                        send(slot(other("frm", d), h, g), other("frm", d), h, g, {"ori": flip(o, b)})
-        nxt = bits[k + 1] if k + 1 < len(bits) else None
+
+    def take(k, g):
         for d in range(nf):
-            for g in range(GROUPS):
-                for h in gained:
-                    arrived(other("frm", d), h, g)
-        held = held + gained
+            for h in held[k][len(held[k]) // 2 :]:
+                arrived(other("frm", d), h, g)
+
+    def later_hop(k, g):
+        take(k, g)
+        if k < len(bits):
+            for d in range(nf):
+                for h in held[k]:
+                    send(slot(other("frm", d), h, g), other("frm", d), h, g, {"ori": flip(o, bits[k])})
+
+    hops = len(bits)
+    for step in range(GROUPS):
+        diffuse(step)
+        first_hop(step)
+        if step >= 1:
+            second_hop(step - 1)
+        if step >= 2:
+            later_hop(1, step - 2)
+    for c in range(early, early + (chunks - early + 1) // 2):
+        slice_chunk(c)
+    second_hop(GROUPS - 1)
+    later_hop(1, GROUPS - 2)
+    for c in range(early + (chunks - early + 1) // 2, chunks):
+        slice_chunk(c)
+    later_hop(1, GROUPS - 1)
+    for k in range(2, hops + 1):
+        for g in range(GROUPS):
+            later_hop(k, g)
 
     tile = 256
-    order = [(nm // 2 + j) % nm for j in range(nm)]
-    order = [q for q in order if q != 0] + [0]
+    order = list(range(nm - 1, -1, -1))
+
+    def target(q):
+        mm, b = m, 1
+        while b < nm:
+            mm = flip(mm, b) if q & b else mm
+            b *= 2
+        return mm
 
     def multiply(ff):
         start = pl.multiple_of(ff * group, group)
@@ -285,39 +304,40 @@
         fd = other("frm", d)
         multiply(fd)
         for q in order:
-            copy = x_copy(f, fd, other("mod", q), n)
+            copy = x_copy(f, fd, target(q), n)
             copy.start()
             pending.append(copy)
             n += 1
     multiply(f)
 
-    def z_copy(src_m, dst_m, n):
+    def z_copy(q):
         return pltpu.make_async_remote_copy(
-            src_ref=part_of(cross, f, dst_m), dst_ref=zrecv.at[src_m],
-            send_sem=zs_sem.at[n], recv_sem=zr_sem.at[src_m],
-            device_id={"mod": dst_m}, device_id_type=MESH,
+            src_ref=part_of(cross, f, target(q)), dst_ref=zrecv.at[q],
+            send_sem=zs_sem.at[q], recv_sem=zr_sem.at[q],
+            device_id={"mod": flip(m, q & -q)}, device_id_type=MESH,
         )
 
     score = None
-    for k, q in enumerate(order):
-        mm = other("mod", q)
+    for q in order:
+        mm = target(q)
         at = pl.ds(pl.multiple_of(f * group + mm * share, share), share)
         value = cross[at, :]
         for d in range(1, nf):
             fd = other("frm", d)
             x_copy(fd, other("frm", 1), mm, 0).wait_recv()
             value = value + xrecv[pl.ds(pl.multiple_of(fd * group + mm * share, share), share), :]
+        b = 1
+        while b < nm and not q & b:
+            z_copy(q | b).wait_recv()
+            value = value + zrecv[q | b]
+            b *= 2
         if q == 0:
             score = value
         else:
             cross[at, :] = value
-            copy = z_copy(m, mm, k)
+            copy = z_copy(q)
             copy.start()
             pending.append(copy)
-    for q in order[:-1]:
-        mm = other("mod", q)
-        z_copy(mm, mm, 0).wait_recv()
-        score = score + zrecv[mm]
     score = score * (1.0 / math.sqrt(rows * nm * lanes))
     peak = jnp.max(score, axis=1, keepdims=True)
     mass = jnp.sum(jnp.exp(score - peak), axis=1, keepdims=True)
@@ -369,7 +389,7 @@
         scratch_shapes=[
             pltpu.VMEM((orient * band, lanes), jnp.int32),
             pltpu.VMEM((orient, depth), bf16),
-            pltpu.VMEM((high, fr, lanes), f32),
+            pltpu.VMEM((high + STRIDE_ROWS, fr, lanes), f32),
             pltpu.VMEM((2, PASSES, fr, lanes), bf16),
             pltpu.VMEM((2, PASSES, fr, lanes), bf16),
             pltpu.VMEM((nf * fr, depth), bf16),

time: 93.2 us -> 78.3 us (0.84)
  Pallas kernels: 90.8 us -> 76.5 us
    pallas_call x1, Pallas kernels: 90.8 us -> 76.5 us  [body(): pl.pallas_call(functools.partial(kernel, dims), out_shape=jax.ShapeDtypeS...]
where the time goes in v2:
time: 78.3 us; the launch traced here: 78.2 us
  Pallas kernels  76.5 us (98%)
  local copies, waits for them, and re-layouts  1.67 us (2%)
    pallas_call x1, Pallas kernels, body(): pl.pallas_call(functools.partial(kernel, dims), out_shape=jax.ShapeDtypeS...  76.5 us
    unnamed x1, local copies, waits for them, and re-layouts  1.67 us

profile of v2, /device:TPU:0, one launch (start us, length us, event | category | flops | bytes accessed | tf_op | source)
XLA Modules:
  0.0 78.2 jit_solution(4215900200186691861)
XLA Ops:
  0.0 76.5 %shard_map.37 = f32[64,1024]{1,0:T(8,128)} custom-call(s32[2048,128]{1,0:T(8,128)} %bitcast.4, s32[16384,128]{1,0:T(8,128)} %bitcast.3, s32[32,128]{1,0:T(8,128)} %mask.1), custom_call_target="tpu_custom_call" | custom-call | tf_op jit(solution)/shard_map/pallas_call | solution.py:384
  76.5 1.7 %copy.5 = f32[1,64,1024]{2,1,0:T(8,128)} copy(f32[1,64,1024]{2,1,0:T(8,128)} %bitcast.5) | data formatting | bytes 524288

commit v3 on v2

--- a/solution.py
+++ b/solution.py
@@ -36,7 +36,7 @@
 
 def kernel(
     dims, counts, codes, mask, out,
-    codes_v, logs, inten, halo_s, halo_r, band_s, frames, cross, xrecv, zrecv,
+    codes_v, logs, inten, halo_s, halo_r, band_s, frames, early_part, cross, xrecv, zrecv,
     stat_s, stat_r, totals,
     code_sem, hs_sem, hr_sem, own_sem, gs_sem, gr_sem, xs_sem, xr_sem, zs_sem, zr_sem,
     ts_sem, tr_sem,
@@ -242,6 +242,43 @@
                 for h in held[k]:
                     send(slot(other("frm", d), h, g), other("frm", d), h, g, {"ori": flip(o, bits[k])})
 
+    tile = 256
+
+    def part_of(ref, ff, mm):
+        return ref.at[pl.ds(ff * group + mm * share, share)]
+
+    per = fr // share if fr % share == 0 else 0
+
+    def x_copy(src_f, dst_f, mm, source=None):
+        return pltpu.make_async_remote_copy(
+            src_ref=part_of(cross, dst_f, mm) if source is None else source,
+            dst_ref=part_of(xrecv, src_f, mm),
+            send_sem=xs_sem.at[dst_f, mm], recv_sem=xr_sem.at[src_f, mm],
+            device_id={"frm": dst_f}, device_id_type=MESH,
+        )
+
+    def early_scores(d):
+        fd = other("frm", d)
+        rows_at = pl.ds(pl.multiple_of((fd * no + o) * fr, fr), fr)
+
+        def one_tile(t, carry):
+            at = pl.multiple_of(t * tile, tile)
+            early_part[pl.ds((d - 1) * fr, fr), pl.ds(at, tile)] = (
+                lax.dot_general(
+                    frames[rows_at, :],
+                    logs[pl.ds(at, tile), :],
+                    (((1,), (1,)), ((), ())),
+                    preferred_element_type=jnp.float32,
+                )
+                - totals[:, pl.ds(at, tile)]
+            )
+            return carry
+
+        lax.fori_loop(0, orient // tile, one_tile, 0)
+        for j in range(per):
+            source = early_part.at[pl.ds((d - 1) * fr + j * share, share)]
+            x_copy(f, fd, o * per + j, source).start()
+
     hops = len(bits)
     for step in range(GROUPS):
         diffuse(step)
@@ -256,12 +293,14 @@
     later_hop(1, GROUPS - 2)
     for c in range(early + (chunks - early + 1) // 2, chunks):
         slice_chunk(c)
+    if per:
+        for d in range(1, nf):
+            early_scores(d)
     later_hop(1, GROUPS - 1)
     for k in range(2, hops + 1):
         for g in range(GROUPS):
             later_hop(k, g)
 
-    tile = 256
     order = list(range(nm - 1, -1, -1))
 
     def target(q):
@@ -289,25 +328,20 @@
 
         lax.fori_loop(0, orient // tile, one_tile, 0)
 
-    def part_of(ref, ff, mm):
-        return ref.at[pl.ds(ff * group + mm * share, share)]
-
-    def x_copy(src_f, dst_f, mm, n):
-        return pltpu.make_async_remote_copy(
-            src_ref=part_of(cross, dst_f, mm), dst_ref=part_of(xrecv, src_f, mm),
-            send_sem=xs_sem.at[n], recv_sem=xr_sem.at[src_f, mm],
-            device_id={"frm": dst_f}, device_id_type=MESH,
-        )
-
-    n = 0
+    def x_start(fd, mm):
+        if not per:
+            x_copy(f, fd, mm).start()
+            return
+
+        @pl.when(mm // per != o)
+        def _():
+            x_copy(f, fd, mm).start()
+
     for d in range(1, nf):
         fd = other("frm", d)
         multiply(fd)
         for q in order:
-            copy = x_copy(f, fd, target(q), n)
-            copy.start()
-            pending.append(copy)
-            n += 1
+            x_start(fd, target(q))
     multiply(f)
 
     def z_copy(q):
@@ -324,7 +358,7 @@
         value = cross[at, :]
         for d in range(1, nf):
             fd = other("frm", d)
-            x_copy(fd, other("frm", 1), mm, 0).wait_recv()
+            x_copy(fd, other("frm", 1), mm).wait_recv()
             value = value + xrecv[pl.ds(pl.multiple_of(fd * group + mm * share, share), share), :]
         b = 1
         while b < nm and not q & b:
@@ -365,6 +399,9 @@
     top = functools.reduce(jnp.maximum, peaks)
     weight = sum(s * jnp.exp(p - top) for p, s in zip(peaks, masses))
     out[...] = score - (top + jnp.log(weight))
+    for d in range(1, nf):
+        for mm in range(nm):
+            x_copy(f, other("frm", d), mm).wait_send()
     for copy in pending:
         copy.wait_send()
 
@@ -394,6 +431,7 @@
             pltpu.VMEM((2, PASSES, fr, lanes), bf16),
             pltpu.VMEM((nf * fr, depth), bf16),
             pltpu.VMEM((nf * group, depth), bf16),
+            pltpu.VMEM((nf * fr, orient), f32),
             pltpu.VMEM((nf * group, orient), f32),
             pltpu.VMEM((nf * group, orient), f32),
             pltpu.VMEM((nm, share, orient), f32),
@@ -406,7 +444,7 @@
             dma((GROUPS,)),
             dma((GROUPS * nf * (no + 1),)),
             dma((nf * no, GROUPS)),
-            dma((nf * nm,)),
+            dma((nf, nm)),
             dma((nf, nm)),
             dma((nm,)),
             dma((nm,)),

time: 78.3 us -> 80.8 us (1.032)
  the two profiles are of different devices: /device:TPU:0 before, /device:TPU:17 now
where the time goes in v3:
time: 80.8 us; the launch traced here: 80.7 us
  Pallas kernels  79 us (98%)
  local copies, waits for them, and re-layouts  1.67 us (2%)
    pallas_call x1, Pallas kernels, body(): pl.pallas_call(functools.partial(kernel, dims), out_shape=jax.ShapeDtypeS...  79 us
    unnamed x1, local copies, waits for them, and re-layouts  1.67 us

profile of v3, /device:TPU:17, one launch (start us, length us, event | category | flops | bytes accessed | tf_op | source)
XLA Modules:
  0.0 80.7 jit_solution(11602644997870711721)
XLA Ops:
  0.0 79.0 %shard_map.37 = f32[64,1024]{1,0:T(8,128)} custom-call(s32[2048,128]{1,0:T(8,128)} %bitcast.4, s32[16384,128]{1,0:T(8,128)} %bitcast.3, s32[32,128]{1,0:T(8,128)} %mask.1), custom_call_target="tpu_custom_call" | custom-call | tf_op jit(solution)/shard_map/pallas_call | solution.py:421
  79.0 1.7 %copy.5 = f32[1,64,1024]{2,1,0:T(8,128)} copy(f32[1,64,1024]{2,1,0:T(8,128)} %bitcast.5) | data formatting | bytes 524288

commit v4 on v2

--- a/solution.py
+++ b/solution.py
@@ -13,7 +13,7 @@
 EDGE_SCALE = 2.0
 LOG_FLOOR = -7.0
 CODE_STEP = 1.0 / 256.0
-GROUPS = 4
+GROUPS = 2
 STRIDE_ROWS = 8
 SLICE_CHUNK = 128
 MESH = pl.DeviceIdType.MESH

time: 78.3 us -> 73.4 us (0.937)
  Pallas kernels: 76.5 us -> 71.6 us
    pallas_call x1, Pallas kernels: 76.5 us -> 71.6 us  [body(): pl.pallas_call(functools.partial(kernel, dims), out_shape=jax.ShapeDtypeS...]
where the time goes in v4:
time: 73.4 us; the launch traced here: 73.2 us
  Pallas kernels  71.6 us (98%)
  local copies, waits for them, and re-layouts  1.67 us (2%)
    pallas_call x1, Pallas kernels, body(): pl.pallas_call(functools.partial(kernel, dims), out_shape=jax.ShapeDtypeS...  71.6 us
    unnamed x1, local copies, waits for them, and re-layouts  1.67 us

profile of v4, /device:TPU:0, one launch (start us, length us, event | category | flops | bytes accessed | tf_op | source)
XLA Modules:
  0.0 73.2 jit_solution(5178958305197278460)
XLA Ops:
  0.0 71.6 %shard_map.37 = f32[64,1024]{1,0:T(8,128)} custom-call(s32[2048,128]{1,0:T(8,128)} %bitcast.4, s32[16384,128]{1,0:T(8,128)} %bitcast.3, s32[32,128]{1,0:T(8,128)} %mask.1), custom_call_target="tpu_custom_call" | custom-call | tf_op jit(solution)/shard_map/pallas_call | solution.py:384
  71.6 1.7 %copy.5 = f32[1,64,1024]{2,1,0:T(8,128)} copy(f32[1,64,1024]{2,1,0:T(8,128)} %bitcast.5) | data formatting | bytes 524288
